TPU v7x, 128 devices: a whole 4x4x4 slice. The times are simulated.
128 devices in a mesh: resp: 32 (over x, z, y_lo), head: 4 (over y_hi, core).
Axes of the slice: x: 4, y: 4 (y_hi: 2, y_lo: 2; y = y_hi * 2 + y_lo), z: 4, core: 2. Of those that a mesh axis runs over, the one named last changes fastest.
Arguments:
- queries: bfloat16 [32, 512, 5120], P('resp', None, 'head'), may hold values from -8 to 8
- resp_keys: bfloat16 [32, 512, 1024], P('resp', None, 'head'), may hold values from -6 to 6
- resp_values: bfloat16 [32, 512, 1024], P('resp', None, 'head'), may hold values from -6 to 6
- prompt_keys: bfloat16 [1024, 1024], P(('resp', 'head')), may hold values from -8 to 8
- prompt_values: bfloat16 [1024, 1024], P(('resp', 'head')), may hold values from -6 to 6
- lengths: int32 [32], P('resp'), may hold values from 64 to 512, as said below
- loss_mask: int32 [32, 512], P('resp'), may hold values 0 or 1
- out_grad: bfloat16 [32, 512, 5120], P('resp', None, 'head'), may hold values from -6 to 6
Outputs:
- attended: bfloat16 [32, 512, 5120], P('resp', None, 'head')
- query_grad: bfloat16 [32, 512, 5120], P('resp', None, 'head')
- key_grad: bfloat16 [32, 512, 1024], P('resp', None, 'head')
- value_grad: bfloat16 [32, 512, 1024], P('resp', None, 'head')
- prompt_key_grad: float32 [1024, 1024], P(('resp', 'head'))
- prompt_value_grad: float32 [1024, 1024], P(('resp', 'head'))
Inputs may be any that keep to these rules, and one draw needn't show every extreme that they name: `lengths`: the longest response has exactly 512 live positions.
All inputs are finite; a program needn't handle non-finite values. No bound on the sum of `loss_mask` on one device may be relied on, other than what follows from the above.
Results may differ from a plain program's by a relative error of at most 0.035.
Values may be sent and summed in bfloat16 or wider, within the bound.
A program may use at most 128 MiB of HBM per device.

v0:
```python
import jax
import jax.numpy as jnp
from jax import lax
from jax.sharding import PartitionSpec as P

HEAD_DIM = 128


def respond(
    query_row, key_row, value_row, length, keep_row, grad_row, prompt_key3, prompt_value3, kv_count
):
    steps_len = query_row.shape[0]
    group_size = query_row.shape[1] // (kv_count * HEAD_DIM)
    score_scale = HEAD_DIM ** (-0.5)
    positions = jnp.arange(steps_len)
    query_five = query_row.reshape(steps_len, kv_count, group_size, HEAD_DIM)
    own_key = key_row.reshape(steps_len, kv_count, HEAD_DIM)
    own_value = value_row.reshape(steps_len, kv_count, HEAD_DIM)
    prompt_scores = (
        jnp.einsum("tkgd,jkd->kgtj", query_five, prompt_key3, preferred_element_type=jnp.float32)
        * score_scale
    )
    own_scores = (
        jnp.einsum("tkgd,jkd->kgtj", query_five, own_key, preferred_element_type=jnp.float32)
        * score_scale
    )
    allowed = (positions[None, :] <= positions[:, None]) & (positions[None, :] < length)
    own_scores = jnp.where(allowed, own_scores, -jnp.inf)
    row_top = jnp.maximum(prompt_scores.max(-1), own_scores.max(-1))
    row_total = jnp.exp(prompt_scores - row_top[..., None]).sum(-1) + jnp.exp(
        own_scores - row_top[..., None]
    ).sum(-1)
    log_total = row_top + jnp.log(row_total)
    prompt_prob = jnp.exp(prompt_scores - log_total[..., None])
    own_prob = jnp.exp(own_scores - log_total[..., None])
    prompt_weight = prompt_prob.astype(jnp.bfloat16)
    own_weight = own_prob.astype(jnp.bfloat16)
    live_rows = positions < length
    attended = jnp.einsum(
        "kgtj,jkd->tkgd", prompt_weight, prompt_value3, preferred_element_type=jnp.float32
    ) + jnp.einsum("kgtj,jkd->tkgd", own_weight, own_value, preferred_element_type=jnp.float32)
    attended = jnp.where(live_rows[:, None, None, None], attended, 0.0).astype(jnp.bfloat16)
    grad_factor = (keep_row * live_rows.astype(jnp.int32)).astype(jnp.bfloat16)
    grad_five = (
        grad_row.reshape(steps_len, kv_count, group_size, HEAD_DIM)
        * grad_factor[:, None, None, None]
    )
    row_delta = jnp.einsum(
        "tkgd,tkgd->kgt", grad_five, attended, preferred_element_type=jnp.float32
    )
    prompt_dprob = jnp.einsum(
        "tkgd,jkd->kgtj", grad_five, prompt_value3, preferred_element_type=jnp.float32
    )
    own_dprob = jnp.einsum(
        "tkgd,jkd->kgtj", grad_five, own_value, preferred_element_type=jnp.float32
    )
    prompt_ds = (prompt_prob * (prompt_dprob - row_delta[..., None]) * score_scale).astype(
        jnp.bfloat16
    )
    own_ds = (own_prob * (own_dprob - row_delta[..., None]) * score_scale).astype(jnp.bfloat16)
    query_grad = jnp.einsum(
        "kgtj,jkd->tkgd", prompt_ds, prompt_key3, preferred_element_type=jnp.float32
    ) + jnp.einsum("kgtj,jkd->tkgd", own_ds, own_key, preferred_element_type=jnp.float32)
    key_grad = jnp.einsum("kgtj,tkgd->jkd", own_ds, query_five, preferred_element_type=jnp.float32)
    value_grad = jnp.einsum(
        "kgtj,tkgd->jkd", own_weight, grad_five, preferred_element_type=jnp.float32
    )
    return (
        attended.reshape(query_row.shape),
        query_grad.astype(jnp.bfloat16).reshape(query_row.shape),
        key_grad.astype(jnp.bfloat16).reshape(key_row.shape),
        value_grad.astype(jnp.bfloat16).reshape(key_row.shape),
        prompt_ds,
        prompt_weight,
        grad_five,
    )


def per_device(
    queries, resp_keys, resp_values, prompt_keys, prompt_values, lengths, loss_mask, out_grad
):
    kv_width = resp_keys.shape[2]
    kv_count = kv_width // HEAD_DIM
    every_key, every_value = (
        lax.all_gather(prompt_keys, ("resp", "head"), axis=0, tiled=True),
        lax.all_gather(prompt_values, ("resp", "head"), axis=0, tiled=True),
    )
    head_start = lax.axis_index("head") * kv_width
    group_keys = lax.dynamic_slice_in_dim(every_key, head_start, kv_width, 1)
    group_values = lax.dynamic_slice_in_dim(every_value, head_start, kv_width, 1)
    prompt_rows = group_keys.shape[0]
    prompt_key3 = group_keys.reshape(prompt_rows, kv_count, HEAD_DIM)
    prompt_value3 = group_values.reshape(prompt_rows, kv_count, HEAD_DIM)

    def one_response(inputs):
        query_row, key_row, value_row, length, keep_row, grad_row = inputs
        return respond(
            query_row,
            key_row,
            value_row,
            length,
            keep_row,
            grad_row,
            prompt_key3,
            prompt_value3,
            kv_count,
        )

    results = lax.map(one_response, (queries, resp_keys, resp_values, lengths, loss_mask, out_grad))
    attended, query_grad, key_grad, value_grad, prompt_ds, prompt_weight, grad_all = results
    query_all = queries.reshape(queries.shape[0], queries.shape[1], kv_count, -1, HEAD_DIM)
    local_rows = prompt_rows // lax.axis_size("resp")
    key_part = jnp.einsum(
        "rkgtj,rtkgd->jkd", prompt_ds, query_all, preferred_element_type=jnp.float32
    )
    value_part = jnp.einsum(
        "rkgtj,rtkgd->jkd", prompt_weight, grad_all, preferred_element_type=jnp.float32
    )
    whole_sum = lax.psum(
        jnp.concatenate(
            [key_part.reshape(prompt_rows, kv_width), value_part.reshape(prompt_rows, kv_width)], 1
        ),
        "resp",
    )
    summed = lax.dynamic_slice_in_dim(whole_sum, lax.axis_index("resp") * local_rows, local_rows, 0)
    key_sum = summed[:, :kv_width]
    value_sum = summed[:, kv_width:]
    prompt_key_grad, prompt_value_grad = (
        lax.all_to_all(key_sum, "head", split_axis=0, concat_axis=1, tiled=True),
        lax.all_to_all(value_sum, "head", split_axis=0, concat_axis=1, tiled=True),
    )
    return (attended, query_grad, key_grad, value_grad, prompt_key_grad, prompt_value_grad)


def solution(mesh):
    placed = (
        P("resp", None, "head"),
        P("resp", None, "head"),
        P("resp", None, "head"),
        P(("resp", "head"), None),
        P(("resp", "head"), None),
        P("resp"),
        P("resp", None),
        P("resp", None, "head"),
    )
    return jax.shard_map(
        per_device,
        mesh=mesh,
        in_specs=placed,
        out_specs=(
            P("resp", None, "head"),
            P("resp", None, "head"),
            P("resp", None, "head"),
            P("resp", None, "head"),
            P(("resp", "head"), None),
            P(("resp", "head"), None),
        ),
        check_vma=False,
    )
```

profile of v0, /device:TPU:1, one launch (start us, length us, event | category | flops | bytes accessed | tf_op | source)
XLA Modules:
  0.0 827.9 jit_solution(10407376835702045725)
XLA Ops:
  8.7 1.6 copy.74
  11.0 1.0 reshape.109
  12.2 2.5 copy.82
  14.7 1.7 reshape.110
  17.3 6.3 fusion.11
  23.6 183.4 %all-gather.3.cloned.1.call-done = bf16[1024,1024]{1,0:T(8,128)(2,1)} async-done(((bf16[8,1024]{1,0:T(8,128)(2,1)}), bf16[1024,1024]{1,0:T(8,128)(2,1)}) %all-gather.3.cloned.1.call-update) | async-done | bytes 2097168 | tf_op jit(solution)/shard_map/all_gather | solution.py:86
  207.0 194.5 %all-gather.5.cloned.1.call-done = bf16[1024,1024]{1,0:T(8,128)(2,1)} async-done(((bf16[8,1024]{1,0:T(8,128)(2,1)}), bf16[1024,1024]{1,0:T(8,128)(2,1)}) %all-gather.5.cloned.1.call-update) | async-done | bytes 2097168 | tf_op jit(solution)/shard_map/all_gather | solution.py:85
  401.5 2.1 constant_dynamic-slice_fusion
  403.6 1.0 copy.145
  404.6 4.0 bitcast_reduce_fusion
  408.6 14.2 %exponential_reduce_fusion = f32[2,5,512]{2,1,0:T(8,128)} fusion(f32[2,512,512,5]{2,1,3,0:T(8,128)} %get-tuple-element.77, f32[2,5,512]{2,1,0:T(8,128)S(1)} %max.11, pred[512,512]{0,1:T(8,128)(4,1)S(1)} %fusion.22), kind=kLoop, calls=%fused_computation.17 | loop fusion | flops 10480640 | bytes 10788864 | tf_op jit(solution)/shard_map/while/body/eval_jaxpr/reduce_sum | solution.py:32
  422.8 3.7 fusion.4
  426.5 12.4 %fusion.16 = f32[2,128,1024,1]{2,1,3,0:T(8,128)} fusion(f32[2,1024,512,5]{2,1,3,0:T(8,128)} %copy-done, f32[2,5,512]{2,1,0:T(8,128)S(1)} %log_add_fusion, bf16[512,2,5,128]{0,3,2,1:T(8,128)(2,1)} %bitcast.152, bf16[512]{0:T(512)(128)(2,1)S(1)} %select_convert_fusion), kind=kOutput, calls=%fused_computation.28 | convolution fusion | flops 1358561280 | bytes 23352320 | tf_op jit(solution)/shard_map/rkgtj,rtkgd->jkd/dot_general | solution.py:116
  439.0 2.7 copy.96
  441.7 2.0 copy.72
  443.7 9.3 %fusion.18 = f32[2,128,5,512]{3,1,2,0:T(8,128)S(1)} fusion(bf16[1024,2,128,1]{0,2,3,1:T(8,128)(2,1)} %bitcast.162, f32[2,1024,512,5]{2,1,3,0:T(8,128)} %copy-done, f32[2,5,512]{2,1,0:T(8,128)S(1)} %log_add_fusion), kind=kOutput, calls=%fused_computation.29 | convolution fusion | flops 1357905920 | bytes 24137728 | tf_op jit(solution)/shard_map/while/body/eval_jaxpr/kgtj,jkd->tkgd/dot_general | solution.py:39
  453.7 4.2 fusion.13
  457.8 13.0 %fusion.2 = bf16[2,5,512,1024]{2,3,1,0:T(8,128)(2,1)} fusion(f32[2,1024,512,5]{2,1,3,0:T(8,128)} %copy-done, f32[2,5,512]{2,1,0:T(8,128)S(1)} %get-tuple-element.78, f32[2,5,512]{2,1,0:T(8,128)S(1)} %log_add_fusion, bf16[1024,2,128,1]{0,2,3,1:T(8,128)(2,1)} %bitcast.163, bf16[512,2,5,128]{0,3,2,1:T(8,128)(2,1)} %bitcast.153, ...), kind=kOutput, calls=%fused_computation.3 | convolution fusion | flops 1376256000 | bytes 33334272 | tf_op jit(solution)/shard_map/while/body/eval_jaxpr/tkgd,jkd->kgtj/dot_general | solution.py:51
  470.8 7.5 fusion.38
  478.3 1.3 copy.95
  479.6 3.3 pad_maximum_fusion
  483.0 7.2 fusion.37
  490.1 7.5 fusion.21
  497.7 5.2 fusion.9
  503.0 270.5 %all-reduce.2.cloned.1.call-done = f32[1024,512]{1,0:T(8,128)} async-done(((f32[1024,512]{1,0:T(8,128)}), f32[1024,512]{1,0:T(8,128)}) %all-reduce.2.cloned.1.call-update) | async-done | bytes 2097168 | tf_op jit(solution)/shard_map/psum | solution.py:119
  773.4 1.4 dynamic-slice_bitcast_fusion
  774.8 26.5 %all-to-all-start = ((f32[4,8,256]{2,1,0:T(8,128)}), f32[4,8,256]{2,1,0:T(8,128)S(1)}, u32[]{:S(2)}, u32[]{:S(2)}) async-start(f32[4,8,256]{2,1,0:T(8,128)} %get-tuple-element.73), calls=%async_computation | async-start | bytes 65536 | tf_op jit(solution)/shard_map/all_to_all | solution.py:129
  801.3 4.2 fusion.12
  806.0 4.3 all-to-all-start.1
  810.3 4.3 fusion.20
  814.6 1.4 copy.98
  817.7 2.4 copy.97
  (60 shorter events, 6.6 us)
Async XLA Ops:
  7.2 199.8 %all-gather.3.cloned.1.call-start = ((), (), s32[]{:S(2)}) async-start(), calls=%async_computation.2 | async-start | bytes 2113536 | tf_op jit(solution)/shard_map/all_gather | solution.py:86
  7.9 393.6 %all-gather.5.cloned.1.call-start = ((), (), s32[]{:S(2)}) async-start(), calls=%async_computation.3 | async-start | bytes 2113536 | tf_op jit(solution)/shard_map/all_gather | solution.py:85
  8.6 764.8 %all-reduce.2.cloned.1.call-start = ((), (), s32[]{:S(2)}) async-start(), calls=%async_computation.4 | async-start | bytes 4194304 | tf_op jit(solution)/shard_map/psum | solution.py:119
  12.2 392.4 %copy-start.7 = (bf16[512,2,128,1]{0,2,3,1:T(8,128)(2,1)}, bf16[512,2,128,1]{0,2,3,1:T(8,128)(2,1)S(1)}, u32[]{:S(2)}) copy-start(bf16[512,2,128,1]{0,2,3,1:T(8,128)(2,1)S(1)} %copy.123) | copy-start | bytes 786436
  17.2 391.4 %copy-start.4 = (pred[512,512]{0,1:T(8,128)(4,1)}, pred[512,512]{0,1:T(8,128)(4,1)S(1)}, u32[]{:S(2)}) copy-start(pred[512,512]{0,1:T(8,128)(4,1)S(1)} %fusion.22) | copy-start | bytes 786436
  404.6 4.0 copy-start.12
  408.6 17.9 %copy-start = (f32[2,1024,512,5]{2,1,3,0:T(8,128)}, f32[2,1024,512,5]{2,1,3,0:T(8,128)S(1)}, u32[]{:S(2)}) copy-start(f32[2,1024,512,5]{2,1,3,0:T(8,128)S(1)} %get-tuple-element.75) | copy-start | bytes 62914564
  422.8 3.7 copy-start.13
  439.0 14.1 %slice-start = ((s8[10485760]{0:T(1024)(128)(4,1)}), s8[2097152]{0:T(1024)(128)(4,1)S(1)}, s32[]{:S(2)}) async-start(s8[10485760]{0:T(1024)(128)(4,1)} %bitcast.144), calls=%async_computation.5 | async-start | bytes 4194304
  443.7 9.4 %slice-start.1 = ((s8[10485760]{0:T(1024)(128)(4,1)}), s8[4194304]{0:T(1024)(128)(4,1)S(1)}, s32[]{:S(2)}) async-start(s8[10485760]{0:T(1024)(128)(4,1)} %bitcast.144), calls=%async_computation.6 | async-start | bytes 8388608
  443.7 9.6 %slice-start.2 = ((s8[10485760]{0:T(1024)(128)(4,1)}), s8[4194304]{0:T(1024)(128)(4,1)S(1)}, s32[]{:S(2)}) async-start(s8[10485760]{0:T(1024)(128)(4,1)} %bitcast.144), calls=%async_computation.7 | async-start | bytes 8388608
  443.7 9.9 %copy-start.1 = (bf16[1,512,1280]{1,2,0:T(8,128)(2,1)S(1)}, bf16[1,512,1280]{1,2,0:T(8,128)(2,1)}, u32[]{:S(2)}) copy-start(bf16[1,512,1280]{1,2,0:T(8,128)(2,1)} %copy.82) | copy-start | bytes 3932164
  443.7 9.9 %copy-start.5 = (pred[512,512]{0,1:T(8,128)(4,1)S(1)}, pred[512,512]{0,1:T(8,128)(4,1)}, u32[]{:S(2)}) copy-start(pred[512,512]{0,1:T(8,128)(4,1)} %copy-done.4) | copy-start | bytes 786436
  443.7 10.0 %copy-start.9 = (bf16[512,2,128]{2,1,0:T(2,128)(2,1)S(1)}, bf16[512,2,128]{2,1,0:T(2,128)(2,1)}, u32[]{:S(2)}) copy-start(bf16[512,2,128]{2,1,0:T(2,128)(2,1)} %reshape.110) | copy-start | bytes 786436
  470.8 12.1 %copy-start.3 = (bf16[1024,256]{0,1:T(8,128)(2,1)S(1)}, bf16[1024,256]{0,1:T(8,128)(2,1)}, u32[]{:S(2)}) copy-start(bf16[1024,256]{0,1:T(8,128)(2,1)} %copy.145) | copy-start | bytes 1572868
  479.6 10.5 %copy-start.2 = (bf16[1,512,1280]{1,2,0:T(8,128)(2,1)S(1)}, bf16[1,512,1280]{1,2,0:T(8,128)(2,1)}, u32[]{:S(2)}) copy-start(bf16[1,512,1280]{1,2,0:T(8,128)(2,1)} %copy.82) | copy-start | bytes 3932164
  479.6 10.5 %copy-start.6 = (pred[512,512]{0,1:T(8,128)(4,1)S(1)}, pred[512,512]{0,1:T(8,128)(4,1)}, u32[]{:S(2)}) copy-start(pred[512,512]{0,1:T(8,128)(4,1)} %copy-done.4) | copy-start | bytes 786436
  482.9 14.7 %slice-start.3 = ((s8[10485760]{0:T(1024)(128)(4,1)}), s8[4194304]{0:T(1024)(128)(4,1)S(1)}, s32[]{:S(2)}) async-start(s8[10485760]{0:T(1024)(128)(4,1)} %bitcast.146), calls=%async_computation.8 | async-start | bytes 8388608
  482.9 14.7 %slice-start.4 = ((s8[10485760]{0:T(1024)(128)(4,1)}), s8[4194304]{0:T(1024)(128)(4,1)S(1)}, s32[]{:S(2)}) async-start(s8[10485760]{0:T(1024)(128)(4,1)} %bitcast.146), calls=%async_computation.9 | async-start | bytes 8388608
  490.1 7.6 slice-start.5
  490.1 7.6 copy-start.10
  497.7 303.6 %copy-start.8 = (bf16[512,2,128,1]{0,2,3,1:T(8,128)(2,1)S(1)}, bf16[512,2,128,1]{0,2,3,1:T(8,128)(2,1)}, u32[]{:S(2)}) copy-start(bf16[512,2,128,1]{0,2,3,1:T(8,128)(2,1)} %copy-done.7) | copy-start | bytes 786436
  502.9 313.9 %copy-start.11 = (bf16[2,128,512]{2,1,0:T(8,128)(2,1)S(1)}, bf16[2,128,512]{2,1,0:T(8,128)(2,1)}, u32[]{:S(2)}) copy-start(bf16[2,128,512]{2,1,0:T(8,128)(2,1)} %fusion.21) | copy-start | bytes 786436
  774.8 31.2 %all-to-all-start = ((f32[4,8,256]{2,1,0:T(8,128)}), f32[4,8,256]{2,1,0:T(8,128)S(1)}, u32[]{:S(2)}, u32[]{:S(2)}) async-start(f32[4,8,256]{2,1,0:T(8,128)} %get-tuple-element.73), calls=%async_computation | async-start | bytes 65536 | tf_op jit(solution)/shard_map/all_to_all | solution.py:129
  806.0 14.1 %all-to-all-start.1 = ((f32[4,8,256]{2,1,0:T(8,128)}), f32[4,8,256]{2,1,0:T(8,128)S(1)}, u32[]{:S(2)}, u32[]{:S(2)}) async-start(f32[4,8,256]{2,1,0:T(8,128)} %get-tuple-element.72), calls=%async_computation.1 | async-start | bytes 65536 | tf_op jit(solution)/shard_map/all_to_all | solution.py:130
Sparse Core Ops, SparseCore 0:
  9.7 197.1 all-gather.2
  208.7 192.7 all-gather.4
  483.0 290.3 all-reduce.1
where the time goes:
time: 829 us; the launch traced here: 828 us
  waiting for transfers between devices  650 us (78%)
  matrix products  85 us (10%)
  starting transfers between devices  30.9 us (4%)
  local copies, waits for them, and re-layouts  25 us (3%)
  other arithmetic  22 us (3%)
  between operations  14.6 us (2%)
    psum x1, waiting for transfers between devices, per_device(): lax.psum(jnp.concatenate([key_part.reshape(prompt_rows, kv_width), value_...  270 us
    all_gather x1, waiting for transfers between devices, per_device(): lax.all_gather(prompt_keys, ('resp', 'head'), axis=0, tiled=True)  195 us
    all_gather x1, waiting for transfers between devices, per_device(): lax.all_gather(prompt_values, ('resp', 'head'), axis=0, tiled=True)  183 us
    all_to_all x1, starting transfers between devices, per_device(): lax.all_to_all(key_sum, 'head', split_axis=0, concat_axis=1, tiled=True)  26.5 us
  transfers between devices with their start and end apart: 5, of which 4 were waited for; matrix products, arithmetic and copies ran while one was open for 6% of the time, Pallas kernels for 0%

commit v1 on v0

--- a/solution.py
+++ b/solution.py
@@ -82,7 +82,12 @@
     kv_width = resp_keys.shape[2]
     kv_count = kv_width // HEAD_DIM
     every_key, every_value = (
-        lax.all_gather(prompt_keys, ("resp", "head"), axis=0, tiled=True),
+        jnp.concatenate(
+            lax.all_to_all(
+                jnp.stack([prompt_keys] * lax.axis_size(("resp", "head"))), ("resp", "head"), 0, 0
+            ),
+            axis=0,
+        ),
         lax.all_gather(prompt_values, ("resp", "head"), axis=0, tiled=True),
     )
     head_start = lax.axis_index("head") * kv_width

time: 829 us -> 648 us (0.78)
  waiting for transfers between devices: 650 us -> 457 us
  starting transfers between devices: 30.9 us -> 42.9 us
    all_gather x1 -> x0, waiting for transfers between devices: 195 us -> none  [per_device(): lax.all_gather(prompt_keys, ('resp', 'head'), axis=0, tiled=True)]
    all_to_all x0 -> x1, waiting for transfers between devices: none -> 18.9 us  [per_device(): lax.all_to_all(jnp.stack([prompt_keys] * lax.axis_size(('resp', 'head')))...]
    all_gather x1, waiting for transfers between devices: 183 us -> 167 us  [per_device(): lax.all_gather(prompt_values, ('resp', 'head'), axis=0, tiled=True)]
    all_to_all x0 -> x1, starting transfers between devices: none -> 12 us  [per_device(): lax.all_to_all(jnp.stack([prompt_keys] * lax.axis_size(('resp', 'head')))...]
  transfers between devices with their start and end apart: 5 -> 5, of which waited for: 4 -> 4; matrix products, arithmetic and copies ran while one was open for 6% -> 7% of each run, Pallas kernels for 0% -> 0%
where the time goes in v1:
time: 648 us; the launch traced here: 647 us
  waiting for transfers between devices  457 us (71%)
  matrix products  85 us (13%)
  starting transfers between devices  42.9 us (7%)
  local copies, waits for them, and re-layouts  25.4 us (4%)
  other arithmetic  21.4 us (3%)
  between operations  15 us (2%)
    psum x1, waiting for transfers between devices, per_device(): lax.psum(jnp.concatenate([key_part.reshape(prompt_rows, kv_width), value_...  271 us
    all_gather x1, waiting for transfers between devices, per_device(): lax.all_gather(prompt_values, ('resp', 'head'), axis=0, tiled=True)  167 us
    all_to_all x1, starting transfers between devices, per_device(): lax.all_to_all(key_sum, 'head', split_axis=0, concat_axis=1, tiled=True)  26.5 us
    all_to_all x1, waiting for transfers between devices, per_device(): lax.all_to_all(jnp.stack([prompt_keys] * lax.axis_size(('resp', 'head')))...  18.9 us
    reduce_sum x1, other arithmetic, respond(): row_total = jnp.exp(prompt_scores - row_top[..., None]).sum(-1) + jnp.exp...  14.2 us
    dot_general x1, matrix products, respond(): jnp.einsum('tkgd,jkd->kgtj', grad_five, prompt_value3, preferred_element_...  13 us
  transfers between devices with their start and end apart: 5, of which 4 were waited for; matrix products, arithmetic and copies ran while one was open for 7% of the time, Pallas kernels for 0%

profile of v1, /device:TPU:1, one launch (start us, length us, event | category | flops | bytes accessed | tf_op | source)
XLA Modules:
  0.0 647.1 jit_solution(5354143130701589052)
XLA Ops:
  7.9 2.3 stack.2
  10.3 12.0 %all-to-all-start = ((bf16[128,8,1024]{2,1,0:T(8,128)(2,1)}), bf16[128,8,1024]{2,1,0:T(8,128)(2,1)}, u32[]{:S(2)}, u32[]{:S(2)}) async-start(bf16[128,8,1024]{2,1,0:T(8,128)(2,1)} %stack.2), calls=%async_computation | async-start | bytes 4194304 | tf_op jit(solution)/shard_map/all_to_all | solution.py:86
  22.3 1.6 copy.74
  24.5 1.0 reshape.115
  25.8 1.5 copy.82
  28.2 6.3 fusion.11
  34.5 18.9 %all-to-all-done = bf16[128,8,1024]{2,1,0:T(8,128)(2,1)} async-done(((bf16[128,8,1024]{2,1,0:T(8,128)(2,1)}), bf16[128,8,1024]{2,1,0:T(8,128)(2,1)}, u32[]{:S(2)}, u32[]{:S(2)}) %all-to-all-start) | async-done | bytes 2097184 | tf_op jit(solution)/shard_map/all_to_all | solution.py:86
  53.4 166.7 %all-gather.2.cloned.1.call-done = bf16[1024,1024]{1,0:T(8,128)(2,1)} async-done(((bf16[8,1024]{1,0:T(8,128)(2,1)}), bf16[1024,1024]{1,0:T(8,128)(2,1)}) %all-gather.2.cloned.1.call-update) | async-done | bytes 2097168 | tf_op jit(solution)/shard_map/all_gather | solution.py:91
  220.1 2.1 constant_dynamic-slice_fusion
  223.2 4.0 bitcast_reduce_fusion
  227.2 14.2 %exponential_reduce_fusion = f32[2,5,512]{2,1,0:T(8,128)} fusion(f32[2,512,512,5]{2,1,3,0:T(8,128)} %get-tuple-element.77, f32[2,5,512]{2,1,0:T(8,128)S(1)} %max.11, pred[512,512]{0,1:T(8,128)(4,1)S(1)} %fusion.22), kind=kLoop, calls=%fused_computation.17 | loop fusion | flops 10480640 | bytes 10788864 | tf_op jit(solution)/shard_map/while/body/eval_jaxpr/reduce_sum | solution.py:32
  241.4 3.7 fusion.4
  245.2 12.4 %fusion.16 = f32[2,128,1024,1]{2,1,3,0:T(8,128)} fusion(f32[2,1024,512,5]{2,1,3,0:T(8,128)} %copy-done, f32[2,5,512]{2,1,0:T(8,128)S(1)} %log_add_fusion, bf16[512,2,5,128]{0,3,2,1:T(8,128)(2,1)} %bitcast.153, bf16[512]{0:T(512)(128)(2,1)S(1)} %select_convert_fusion), kind=kOutput, calls=%fused_computation.28 | convolution fusion | flops 1358561280 | bytes 23352320 | tf_op jit(solution)/shard_map/rkgtj,rtkgd->jkd/dot_general | solution.py:121
  257.6 2.7 copy.96
  260.3 2.0 copy.72
  262.3 9.3 %fusion.18 = f32[2,128,5,512]{3,1,2,0:T(8,128)S(1)} fusion(bf16[1024,2,128,1]{0,2,3,1:T(8,128)(2,1)} %bitcast.163, f32[2,1024,512,5]{2,1,3,0:T(8,128)} %copy-done, f32[2,5,512]{2,1,0:T(8,128)S(1)} %log_add_fusion), kind=kOutput, calls=%fused_computation.29 | convolution fusion | flops 1357905920 | bytes 24137728 | tf_op jit(solution)/shard_map/while/body/eval_jaxpr/kgtj,jkd->tkgd/dot_general | solution.py:39
  272.3 4.2 fusion.13
  276.5 13.0 %fusion.2 = bf16[2,5,512,1024]{2,3,1,0:T(8,128)(2,1)} fusion(f32[2,1024,512,5]{2,1,3,0:T(8,128)} %copy-done, f32[2,5,512]{2,1,0:T(8,128)S(1)} %get-tuple-element.78, f32[2,5,512]{2,1,0:T(8,128)S(1)} %log_add_fusion, bf16[1024,2,128,1]{0,2,3,1:T(8,128)(2,1)} %bitcast.164, bf16[512,2,5,128]{0,3,2,1:T(8,128)(2,1)} %bitcast.154, ...), kind=kOutput, calls=%fused_computation.3 | convolution fusion | flops 1376256000 | bytes 33334272 | tf_op jit(solution)/shard_map/while/body/eval_jaxpr/tkgd,jkd->kgtj/dot_general | solution.py:51
  289.4 7.5 %fusion.38 = f32[2,1024,128,1]{1,2,3,0:T(8,128)S(1)} fusion(bf16[2,5,512,1024]{2,3,1,0:T(8,128)(2,1)} %fusion.2, bf16[512,2,5,128]{0,3,2,1:T(8,128)(2,1)S(1)} %bitcast.151), kind=kOutput, calls=%fused_computation.56 | convolution fusion | flops 1342177280 | bytes 12845056 | tf_op jit(solution)/shard_map/rkgtj,rtkgd->jkd/dot_general | solution.py:118
  296.9 1.3 copy.95
  298.2 3.3 pad_maximum_fusion
  301.6 7.2 %fusion.37 = f32[2,128,5,512]{3,1,2,0:T(8,128)} fusion(bf16[1024,2,128,1]{0,2,3,1:T(8,128)(2,1)S(1)} %bitcast.160, bf16[2,5,512,1024]{2,3,1,0:T(8,128)(2,1)} %fusion.2), kind=kOutput, calls=%fused_computation.55 | convolution fusion | flops 1342177280 | bytes 13631488 | tf_op jit(solution)/shard_map/while/body/eval_jaxpr/kgtj,jkd->tkgd/dot_general | solution.py:61
  308.8 7.6 %fusion.21 = bf16[2,128,512]{2,1,0:T(8,128)(2,1)} fusion(bf16[512,2,5,128]{0,3,2,1:T(8,128)(2,1)S(1)} %bitcast.156, bf16[512]{0:T(512)(128)(2,1)S(1)} %select_convert_fusion, f32[2,512,512,5]{2,1,3,0:T(8,128)} %get-tuple-element.77, f32[2,5,512]{2,1,0:T(8,128)S(1)} %log_add_fusion, pred[512,512]{0,1:T(8,128)(4,1)S(1)} %copy-done.6), kind=kOutput, calls=%fused_computation.33 | convolution fusion | flops 682360832 | bytes 12342272 | tf_op jit(solution)/shard_map/while/body/eval_jaxpr/kgtj,tkgd->jkd/dot_general | solution.py:65
  316.4 5.2 fusion.9
  321.6 270.7 %all-reduce.2.cloned.1.call-done = f32[1024,512]{1,0:T(8,128)} async-done(((f32[1024,512]{1,0:T(8,128)}), f32[1024,512]{1,0:T(8,128)}) %all-reduce.2.cloned.1.call-update) | async-done | bytes 2097168 | tf_op jit(solution)/shard_map/psum | solution.py:124
  592.3 1.4 dynamic-slice_bitcast_fusion
  593.7 26.5 %all-to-all-start.1 = ((f32[4,8,256]{2,1,0:T(8,128)}), f32[4,8,256]{2,1,0:T(8,128)S(1)}, u32[]{:S(2)}, u32[]{:S(2)}) async-start(f32[4,8,256]{2,1,0:T(8,128)} %get-tuple-element.73), calls=%async_computation.1 | async-start | bytes 65536 | tf_op jit(solution)/shard_map/all_to_all | solution.py:134
  620.2 4.2 fusion.12
  624.9 4.3 all-to-all-start.2
  629.2 4.3 fusion.20
  633.5 1.4 copy.98
  636.6 2.4 copy.97
  (66 shorter events, 7.0 us)
Async XLA Ops:
  7.2 18.6 %copy-start.9 = (bf16[1,512,1280]{2,1,0:T(8,128)(2,1)S(1)}, bf16[1,512,1280]{2,1,0:T(8,128)(2,1)}, u32[]{:S(2)}) copy-start(bf16[1,512,1280]{2,1,0:T(8,128)(2,1)} %param.15) | copy-start | bytes 3932164
  7.2 20.1 %copy-start.10 = (bf16[1,512,256]{2,1,0:T(8,128)(2,1)S(1)}, bf16[1,512,256]{2,1,0:T(8,128)(2,1)}, u32[]{:S(2)}) copy-start(bf16[1,512,256]{2,1,0:T(8,128)(2,1)} %param.10) | copy-start | bytes 786436
  7.2 20.8 %copy-start.16 = (s32[1,512]{1,0:T(1,128)S(1)}, s32[1,512]{1,0:T(1,128)}, u32[]{:S(2)}) copy-start(s32[1,512]{1,0:T(1,128)} %param.14) | copy-start | bytes 6148
  7.2 212.9 %all-gather.2.cloned.1.call-start = ((), (), s32[]{:S(2)}) async-start(), calls=%async_computation.3 | async-start | bytes 2113536 | tf_op jit(solution)/shard_map/all_gather | solution.py:91
  10.3 43.2 %all-to-all-start = ((bf16[128,8,1024]{2,1,0:T(8,128)(2,1)}), bf16[128,8,1024]{2,1,0:T(8,128)(2,1)}, u32[]{:S(2)}, u32[]{:S(2)}) async-start(bf16[128,8,1024]{2,1,0:T(8,128)(2,1)} %stack.2), calls=%async_computation | async-start | bytes 4194304 | tf_op jit(solution)/shard_map/all_to_all | solution.py:86
  22.2 570.1 %all-reduce.2.cloned.1.call-start = ((), (), s32[]{:S(2)}) async-start(), calls=%async_computation.4 | async-start | bytes 4194304 | tf_op jit(solution)/shard_map/psum | solution.py:124
  25.8 197.4 %copy-start.7 = (bf16[512,2,128,1]{0,2,3,1:T(8,128)(2,1)}, bf16[512,2,128,1]{0,2,3,1:T(8,128)(2,1)S(1)}, u32[]{:S(2)}) copy-start(bf16[512,2,128,1]{0,2,3,1:T(8,128)(2,1)S(1)} %copy.123) | copy-start | bytes 786436
  28.2 199.0 %copy-start.4 = (pred[512,512]{0,1:T(8,128)(4,1)}, pred[512,512]{0,1:T(8,128)(4,1)S(1)}, u32[]{:S(2)}) copy-start(pred[512,512]{0,1:T(8,128)(4,1)S(1)} %fusion.22) | copy-start | bytes 786436
  223.2 4.0 copy-start.14
  227.2 17.9 %copy-start = (f32[2,1024,512,5]{2,1,3,0:T(8,128)}, f32[2,1024,512,5]{2,1,3,0:T(8,128)S(1)}, u32[]{:S(2)}) copy-start(f32[2,1024,512,5]{2,1,3,0:T(8,128)S(1)} %get-tuple-element.75) | copy-start | bytes 62914564
  241.4 3.7 copy-start.15
  257.6 14.1 %slice-start = ((s8[10485760]{0:T(1024)(128)(4,1)}), s8[2097152]{0:T(1024)(128)(4,1)S(1)}, s32[]{:S(2)}) async-start(s8[10485760]{0:T(1024)(128)(4,1)} %bitcast.145), calls=%async_computation.5 | async-start | bytes 4194304
  262.3 9.4 %slice-start.1 = ((s8[10485760]{0:T(1024)(128)(4,1)}), s8[4194304]{0:T(1024)(128)(4,1)S(1)}, s32[]{:S(2)}) async-start(s8[10485760]{0:T(1024)(128)(4,1)} %bitcast.145), calls=%async_computation.6 | async-start | bytes 8388608
  262.3 9.6 %slice-start.2 = ((s8[10485760]{0:T(1024)(128)(4,1)}), s8[4194304]{0:T(1024)(128)(4,1)S(1)}, s32[]{:S(2)}) async-start(s8[10485760]{0:T(1024)(128)(4,1)} %bitcast.145), calls=%async_computation.7 | async-start | bytes 8388608
  262.3 9.9 %copy-start.1 = (bf16[1,512,1280]{1,2,0:T(8,128)(2,1)S(1)}, bf16[1,512,1280]{1,2,0:T(8,128)(2,1)}, u32[]{:S(2)}) copy-start(bf16[1,512,1280]{1,2,0:T(8,128)(2,1)} %copy.82) | copy-start | bytes 3932164
  262.3 9.9 %copy-start.5 = (pred[512,512]{0,1:T(8,128)(4,1)S(1)}, pred[512,512]{0,1:T(8,128)(4,1)}, u32[]{:S(2)}) copy-start(pred[512,512]{0,1:T(8,128)(4,1)} %copy-done.4) | copy-start | bytes 786436
  262.3 10.0 %copy-start.11 = (bf16[512,2,128]{2,1,0:T(2,128)(2,1)S(1)}, bf16[512,2,128]{2,1,0:T(2,128)(2,1)}, u32[]{:S(2)}) copy-start(bf16[512,2,128]{2,1,0:T(2,128)(2,1)} %reshape.116) | copy-start | bytes 786436
  289.4 12.1 %copy-start.3 = (bf16[1024,256]{0,1:T(8,128)(2,1)S(1)}, bf16[1024,256]{0,1:T(8,128)(2,1)}, u32[]{:S(2)}) copy-start(bf16[1024,256]{0,1:T(8,128)(2,1)} %copy.73) | copy-start | bytes 1572868
  298.2 10.6 %copy-start.2 = (bf16[1,512,1280]{1,2,0:T(8,128)(2,1)S(1)}, bf16[1,512,1280]{1,2,0:T(8,128)(2,1)}, u32[]{:S(2)}) copy-start(bf16[1,512,1280]{1,2,0:T(8,128)(2,1)} %copy.82) | copy-start | bytes 3932164
  298.2 10.6 %copy-start.6 = (pred[512,512]{0,1:T(8,128)(4,1)S(1)}, pred[512,512]{0,1:T(8,128)(4,1)}, u32[]{:S(2)}) copy-start(pred[512,512]{0,1:T(8,128)(4,1)} %copy-done.4) | copy-start | bytes 786436
  301.6 14.8 %slice-start.3 = ((s8[10485760]{0:T(1024)(128)(4,1)}), s8[4194304]{0:T(1024)(128)(4,1)S(1)}, s32[]{:S(2)}) async-start(s8[10485760]{0:T(1024)(128)(4,1)} %bitcast.147), calls=%async_computation.8 | async-start | bytes 8388608
  301.6 14.8 %slice-start.4 = ((s8[10485760]{0:T(1024)(128)(4,1)}), s8[4194304]{0:T(1024)(128)(4,1)S(1)}, s32[]{:S(2)}) async-start(s8[10485760]{0:T(1024)(128)(4,1)} %bitcast.147), calls=%async_computation.9 | async-start | bytes 8388608
  308.8 7.6 %slice-start.5 = ((s8[10485760]{0:T(1024)(128)(4,1)}), s8[2097152]{0:T(1024)(128)(4,1)S(1)}, s32[]{:S(2)}) async-start(s8[10485760]{0:T(1024)(128)(4,1)} %bitcast.147), calls=%async_computation.10 | async-start | bytes 4194304
  308.8 7.6 %copy-start.12 = (bf16[512,2,128]{2,1,0:T(2,128)(2,1)S(1)}, bf16[512,2,128]{2,1,0:T(2,128)(2,1)}, u32[]{:S(2)}) copy-start(bf16[512,2,128]{2,1,0:T(2,128)(2,1)} %reshape.116) | copy-start | bytes 786436
  316.4 303.9 %copy-start.8 = (bf16[512,2,128,1]{0,2,3,1:T(8,128)(2,1)S(1)}, bf16[512,2,128,1]{0,2,3,1:T(8,128)(2,1)}, u32[]{:S(2)}) copy-start(bf16[512,2,128,1]{0,2,3,1:T(8,128)(2,1)} %copy-done.7) | copy-start | bytes 786436
  321.6 314.2 %copy-start.13 = (bf16[2,128,512]{2,1,0:T(8,128)(2,1)S(1)}, bf16[2,128,512]{2,1,0:T(8,128)(2,1)}, u32[]{:S(2)}) copy-start(bf16[2,128,512]{2,1,0:T(8,128)(2,1)} %fusion.21) | copy-start | bytes 786436
  593.7 31.2 %all-to-all-start.1 = ((f32[4,8,256]{2,1,0:T(8,128)}), f32[4,8,256]{2,1,0:T(8,128)S(1)}, u32[]{:S(2)}, u32[]{:S(2)}) async-start(f32[4,8,256]{2,1,0:T(8,128)} %get-tuple-element.73), calls=%async_computation.1 | async-start | bytes 65536 | tf_op jit(solution)/shard_map/all_to_all | solution.py:134
  624.9 14.2 %all-to-all-start.2 = ((f32[4,8,256]{2,1,0:T(8,128)}), f32[4,8,256]{2,1,0:T(8,128)S(1)}, u32[]{:S(2)}, u32[]{:S(2)}) async-start(f32[4,8,256]{2,1,0:T(8,128)} %get-tuple-element.72), calls=%async_computation.2 | async-start | bytes 65536 | tf_op jit(solution)/shard_map/all_to_all | solution.py:135
Sparse Core Ops, SparseCore 0:
  9.8 210.3 all-gather.1
  301.7 290.5 all-reduce.1
